TPU v7x, 32 devices: a whole 2x2x4 slice. The times are simulated.
32 devices in a mesh: shot: 16 (over z, x, core), freq: 2 (over y).
Axes of the slice: x: 2, y: 2, z: 4, core: 2. Of those that a mesh axis runs over, the one named last changes fastest.
Arguments:
- wavefield: bfloat16 [4, 6144, 1024], P('freq', 'shot'), parts along dimension 0, may hold values from -0.8984375 to 0.8984375
- recorded: bfloat16 [6, 2, 2, 6144, 384], P('freq', None, None, 'shot'), parts along dimension 0, may hold values from -6 to 6
- match_filter: bfloat16 [2, 63], replicated, may hold values from -0.5 to 0.5
Outputs:
- demultiple: bfloat16 [6, 2, 2, 6144, 384], P('freq', None, None, 'shot'), parts along dimension 0
There are 2 independent parts, one for each index of `freq`. A program takes and returns all parts, laid end to end along the dimension named above; an argument that names none is the same for every part. Nothing has to cross between parts.
All inputs are finite; a program needn't handle non-finite values.
Results may differ from a plain program's by a relative error of at most 0.0048.
Values may be sent and summed in bfloat16 or wider, within the bound.
A program may use at most 64 MiB of HBM per device.

v0:
```python
import functools

import jax
import jax.numpy as jnp
from jax import lax
from jax.experimental import pallas as pl
from jax.experimental.pallas import tpu as pltpu
from jax.sharding import PartitionSpec as P

MESH = pl.DeviceIdType.MESH
STEP = 128
CH_A, CH_B, CH_C, CH_M, CH_D, CH_TA, CH_TX = range(7)
LIMIT = 40 * 2**20
F32 = jnp.float32
BF16 = jnp.bfloat16


def dot_t(a, b):
    return lax.dot_general(a, b, (((1,), (1,)), ((), ())), preferred_element_type=F32)


def kernel(
    n, mf_hbm, wave, rec, out,
    mf, wave_v, left, weights, buf_a, buf_b, buf_c, buf_m, buf_d,
    send_a, send_x, recv_a, recv_x, tile, tile2, tile3, rec_v, res, taps_row,
    ssem, rsem, in_sem, out_sem,
):
    span, depth = wave_v.shape[1], wave_v.shape[2]
    pieces = span // STEP
    half = (mf.shape[1] - 1) // 2
    me = lax.axis_index("shot")
    core = lax.rem(me, 2)
    side = lax.rem(me // 2, 2)
    mate = me + 1 - 2 * core
    across = me + 2 - 4 * side
    beyond = lax.rem(me + n - 2 + 4 * side, n)
    up, down = lax.rem(me + 4, n), lax.rem(me + n - 4, n)
    z_to = (1 - side) * down + side * up
    z_from = (1 - side) * up + side * down
    owner = (core == side)
    giver = (core != side)

    load_taps = pltpu.make_async_copy(mf_hbm, mf, in_sem.at[2])
    load_taps.start()
    load_wave = pltpu.make_async_copy(wave, wave_v, in_sem.at[0])
    load_wave.start()
    load = pltpu.make_async_copy(rec, rec_v, in_sem.at[1])
    load.start()

    barrier = pltpu.get_barrier_semaphore()
    for other in (mate, across, beyond, up, down):
        pl.semaphore_signal(barrier, inc=1, device_id={"shot": other}, device_id_type=MESH)
    pl.semaphore_wait(barrier, 5)

    def remote(src, dst, sem, target):
        return pltpu.make_async_remote_copy(
            src_ref=src, dst_ref=dst, send_sem=ssem.at[sem], recv_sem=rsem.at[sem],
            device_id={"shot": target}, device_id_type=MESH,
        )

    def rows(i):
        if isinstance(i, int):
            return pl.ds(i * STEP, STEP)
        return pl.ds(pl.multiple_of(i * STEP, STEP), STEP)

    def cols(i, base):
        return pl.ds(pl.multiple_of(base + i * STEP, STEP), STEP)

    def piece(src, dst, channel, i, target):
        return remote(
            src.at[:, rows(i), :], dst.at[:, rows(i), :], channel * pieces + i, target
        )

    def tile_piece(src, dst, channel, i, target):
        return remote(src.at[rows(i), :], dst.at[rows(i), :], channel * pieces + i, target)

    def z_copy(i):
        return piece(wave, buf_a, CH_A, i, z_to)

    def fwd_copy(i):
        return piece(buf_a, buf_b, CH_B, i, across)

    def row_copy(i):
        return piece(wave, buf_c, CH_C, i, across)

    def mate_copy(i):
        return piece(wave, buf_m, CH_M, i, mate)

    def share_c(i):
        return piece(buf_c, buf_d, CH_D, i, mate)

    def share_b(i):
        return piece(buf_b, buf_d, CH_D, i, mate)

    def tile_a(i):
        return tile_piece(send_a, recv_a, CH_TA, i, z_from)

    def tile_b(i):
        return tile_piece(send_x, recv_x, CH_TX, i, beyond)

    def tile_c(i):
        return tile_piece(send_x, recv_x, CH_TX, i, across)

    @pl.when(giver)
    def _():
        for i in range(pieces):
            row_copy(i).start()

    for i in range(pieces):
        z_copy(i).start()
    for i in range(pieces):
        mate_copy(i).start()

    load_taps.wait()
    width = taps_row.shape[1]
    taps_row[...] = jnp.zeros_like(taps_row)
    taps_row[0:2, 0:mf.shape[1]] = mf[...].astype(F32)
    row_id = lax.broadcasted_iota(jnp.int32, (span, width), 0)
    banded = []
    for c in range(2):
        x = jnp.broadcast_to(taps_row[c:c + 1, :], (span, width))
        x = pltpu.roll(x, width - half, 1)
        bit = 1
        while bit < span:
            x = jnp.where((row_id // bit) % 2 == 1, pltpu.roll(x, bit, 1), x)
            bit *= 2
        banded.append(x[:, :span].astype(BF16))
    weights[:span, :span] = banded[0]
    weights[:span, span:] = -banded[1]
    weights[span:, :span] = banded[1]
    weights[span:, span:] = banded[0]

    load_wave.wait()
    left[:span, :depth] = wave_v[0]
    left[:span, depth:] = -wave_v[1]
    left[span:, :depth] = wave_v[1]
    left[span:, depth:] = wave_v[0]

    def own_tile(src, dst, i):
        t = dot_t(left[:, :depth], src[0, rows(i), :]) + dot_t(left[:, depth:], src[1, rows(i), :])
        t = t.astype(BF16)
        dst[:, cols(i, 0)] = t[:span]
        dst[:, cols(i, span)] = t[span:]

    def their_tile(src, dst, i):
        t = dot_t(src[0, rows(i), :], left[:, :depth]) + dot_t(src[1, rows(i), :], left[:, depth:])
        dst[rows(i), :] = t.astype(BF16)

    def put(t, k, i, j):
        return pltpu.make_async_copy(
            res.at[t, k, :, rows(i), :], out.at[t, k, :, rows(i), :], out_sem.at[j * pieces + i]
        )

    def emit(t, k, src, i, j):
        f = dot_t(src[rows(i), :], weights[...])
        res[t, k, 0, rows(i), :] = (rec_v[t, k, 0, rows(i), :].astype(F32) - f[:, :span]).astype(BF16)
        res[t, k, 1, rows(i), :] = (rec_v[t, k, 1, rows(i), :].astype(F32) - f[:, span:]).astype(BF16)
        put(t, k, i, j).start()

    def each(body):
        def step(i, carry):
            body(i)
            return carry
        lax.fori_loop(0, pieces, step, 0)

    load.wait()

    @each
    def _(i):
        mate_copy(i).wait_recv()
        own_tile(buf_m, tile, i)

    each(lambda i: emit(0, core, tile, i, 0))

    @pl.when(owner)
    def _():
        @each
        def _(i):
            row_copy(i).wait_recv()
            share_c(i).start()
            z_copy(i).wait_recv()
            fwd_copy(i).start()
            their_tile(buf_c, send_x, i)
            tile_c(i).start()
            their_tile(buf_a, send_a, i)

            @pl.when(i == pieces - 1)
            def _():
                for j in range(pieces):
                    tile_a(j).start()

            own_tile(buf_c, tile3, i)
            own_tile(buf_a, tile, i)

        @each
        def _(i):
            emit(1, side, tile3, i, 3)
            emit(2, side, tile, i, 1)

        @each
        def _(i):
            share_b(i).wait_recv()
            own_tile(buf_d, tile2, i)

        each(lambda i: emit(0, 1 - core, tile2, i, 4))

        @each
        def _(i):
            tile_a(i).wait_recv()
            emit(2, 1 - side, recv_a, i, 5)
            tile_b(i).wait_recv()
            emit(1, 1 - side, recv_x, i, 2)

        @each
        def _(i):
            share_c(i).wait_send()
            fwd_copy(i).wait_send()
            tile_c(i).wait_send()

    @pl.when(giver)
    def _():
        @each
        def _(i):
            z_copy(i).wait_recv()
            their_tile(buf_a, send_a, i)

            @pl.when(i == pieces - 1)
            def _():
                for j in range(pieces):
                    tile_a(j).start()

            own_tile(buf_a, tile, i)
            share_c(i).wait_recv()
            own_tile(buf_d, tile3, i)
            fwd_copy(i).wait_recv()
            share_b(i).start()
            their_tile(buf_b, send_x, i)
            tile_b(i).start()
            own_tile(buf_b, tile2, i)

        @each
        def _(i):
            emit(2, side, tile, i, 1)
            emit(0, 1 - core, tile3, i, 4)
            emit(1, 1 - side, tile2, i, 2)

        @each
        def _(i):
            tile_c(i).wait_recv()
            emit(1, side, recv_x, i, 3)

        @each
        def _(i):
            tile_a(i).wait_recv()
            emit(2, 1 - side, recv_a, i, 5)

        @each
        def _(i):
            row_copy(i).wait_send()
            share_b(i).wait_send()
            tile_b(i).wait_send()

    @each
    def _(i):
        z_copy(i).wait_send()
        mate_copy(i).wait_send()
        tile_a(i).wait_send()
        put(0, core, i, 0).wait()
        put(2, side, i, 1).wait()
        put(1, 1 - side, i, 2).wait()
        put(1, side, i, 3).wait()
        put(0, 1 - core, i, 4).wait()
        put(2, 1 - side, i, 5).wait()


def ladder(wavefield, recorded, match_filter):
    n = lax.axis_size("shot")
    _, span, depth = wavefield.shape
    pieces = span // STEP
    slots = recorded.shape[0]
    width = -(-(span + match_filter.shape[1]) // STEP) * STEP
    block = pltpu.VMEM((2, span, depth), BF16)
    flat = pltpu.VMEM((span, 2 * span), BF16)
    return pl.pallas_call(
        functools.partial(kernel, n),
        out_shape=jax.ShapeDtypeStruct(recorded.shape, recorded.dtype),
        in_specs=[
            pl.BlockSpec(memory_space=pltpu.HBM),
            pl.BlockSpec(memory_space=pltpu.HBM),
            pl.BlockSpec(memory_space=pltpu.HBM),
        ],
        out_specs=pl.BlockSpec(memory_space=pl.ANY),
        scratch_shapes=[
            pltpu.VMEM(match_filter.shape, BF16),
            block,
            pltpu.VMEM((2 * span, 2 * depth), BF16),
            pltpu.VMEM((2 * span, 2 * span), BF16),
            block, block, block, block, block,
            flat, flat, flat, flat, flat, flat, flat,
            pltpu.VMEM(recorded.shape, BF16),
            pltpu.VMEM(recorded.shape, BF16),
            pltpu.VMEM((8, width), F32),
            pltpu.SemaphoreType.DMA((7 * pieces,)),
            pltpu.SemaphoreType.DMA((7 * pieces,)),
            pltpu.SemaphoreType.DMA((3,)),
            pltpu.SemaphoreType.DMA((2 * slots * pieces,)),
        ],
        compiler_params=pltpu.CompilerParams(
            collective_id=0, has_side_effects=True, vmem_limit_bytes=LIMIT
        ),
    )(*(pltpu.with_memory_space_constraint(x, pltpu.HBM) for x in (match_filter, wavefield, recorded)))


def passed_along(value, axis, steps):
    count = lax.axis_size(axis)
    pairs = [(source, (source + steps) % count) for source in range(count)]
    return lax.ppermute(value, axis, pairs)


def toeplitz(match_filter, block_span_width):
    tap_count = match_filter.shape[1]
    half_taps = (tap_count - 1) // 2
    row_index = lax.broadcasted_iota(jnp.int32, (block_span_width, block_span_width), 0)
    col_index = lax.broadcasted_iota(jnp.int32, (block_span_width, block_span_width), 1)
    lag_index = row_index - col_index + half_taps
    coeffs = match_filter.astype(jnp.float32)

    def place_tap(tap_index, carried):
        column = lax.dynamic_slice_in_dim(coeffs, tap_index, 1, 1)
        return jnp.where((lag_index == tap_index)[None], column[:, :, None], carried)

    return lax.fori_loop(
        0, tap_count, place_tap, jnp.zeros((2, block_span_width, block_span_width), jnp.float32)
    )


def filter_weights(match_filter, block_span_width):
    toe_pair = toeplitz(match_filter, block_span_width)
    real_component = toe_pair[0].astype(jnp.bfloat16)
    imag_part = toe_pair[1].astype(jnp.bfloat16)
    return jnp.stack(
        [jnp.stack([real_component, imag_part], 1), jnp.stack([-imag_part, real_component], 1)], 0
    )


def shards(wavefield, recorded, match_filter):
    cycle_size = lax.axis_size("shot")
    doubling = cycle_size // 8 == 2 and cycle_size // 4 == 4
    if doubling and cycle_size % 4 == 0 and wavefield.shape[1] % STEP == 0:
        return ladder(wavefield, recorded, match_filter)
    block_span_width = wavefield.shape[1]
    weights = filter_weights(match_filter, block_span_width)
    real_component = wavefield[0]
    imag_part = wavefield[1]
    left_rows = jnp.concatenate(
        [
            jnp.concatenate([real_component, -imag_part], 1),
            jnp.concatenate([imag_part, real_component], 1),
        ],
        0,
    )
    results = []
    for slot_index, offset in enumerate((1, cycle_size // 8, cycle_size // 4)):
        ahead_data = passed_along(wavefield, "shot", -offset)
        right_rows = jnp.concatenate([ahead_data[0], ahead_data[1]], 1)
        stacked = lax.dot_general(
            left_rows, right_rows, (((1,), (1,)), ((), ())), preferred_element_type=jnp.float32
        )
        forward_tile = stacked.astype(jnp.bfloat16).reshape(2, block_span_width, block_span_width)
        ahead_filtered = jnp.einsum(
            "csq,cqdx->dsx", forward_tile, weights, preferred_element_type=jnp.float32
        )
        received = passed_along(forward_tile, "shot", offset)
        behind_filtered = jnp.einsum(
            "csr,csdx->drx", received, weights, preferred_element_type=jnp.float32
        )
        ahead_out = (recorded[slot_index, 0].astype(jnp.float32) - ahead_filtered).astype(
            jnp.bfloat16
        )
        behind_out = (recorded[slot_index, 1].astype(jnp.float32) - behind_filtered).astype(
            jnp.bfloat16
        )
        results.append(jnp.stack([ahead_out, behind_out]))
    return jnp.stack(results)


def solution(mesh):
    return jax.shard_map(
        shards,
        mesh=mesh,
        in_specs=(P("freq", "shot", None), P("freq", None, None, "shot", None), P()),
        out_specs=P("freq", None, None, "shot", None),
        check_vma=False,
    )
```

profile of v0, /device:TPU:1, one launch (start us, length us, event | category | flops | bytes accessed | tf_op | source)
XLA Modules:
  0.0 66.6 jit_solution(10544176696651857831)
XLA Ops:
  0.0 64.8 %shard_map.37 = bf16[3,2,2,384,384]{4,3,2,1,0:T(8,128)(2,1)S(1)} custom-call(bf16[2,63]{1,0:T(2,128)(2,1)} %mf_hbm.1, bf16[2,384,1024]{2,1,0:T(8,128)(2,1)} %wave.1, bf16[3,2,2,384,384]{4,3,2,1,0:T(8,128)(2,1)} %rec.1), custom_call_target="tpu_custom_call" | custom-call | tf_op jit(solution)/shard_map/pallas_call | solution.py:284
  64.8 1.8 %copy.5 = bf16[3,2,2,384,384]{4,3,2,1,0:T(8,128)(2,1)} copy(bf16[3,2,2,384,384]{4,3,2,1,0:T(8,128)(2,1)S(1)} %shard_map.37) | data formatting | bytes 7077888
where the time goes:
time: 66.8 us; the launch traced here: 66.6 us
  Pallas kernels  64.8 us (97%)
  local copies, waits for them, and re-layouts  1.8 us (3%)
    pallas_call x1, Pallas kernels, ladder(): pl.pallas_call(functools.partial(kernel, n), out_shape=jax.ShapeDtypeStru...  64.8 us
    unnamed x1, local copies, waits for them, and re-layouts  1.8 us

commit v1 on v0

v1 whole, which is shorter than its diff:
```python
import functools

import jax
import jax.numpy as jnp
from jax import lax
from jax.experimental import pallas as pl
from jax.experimental.pallas import tpu as pltpu
from jax.sharding import PartitionSpec as P

MESH = pl.DeviceIdType.MESH
STEP = 128
CH_X, CH_Z, CH_M, CH_D, CH_A, CH_C, CH_O = range(7)
LIMIT = 40 * 2**20
F32 = jnp.float32
BF16 = jnp.bfloat16


def dot_t(a, b):
    return lax.dot_general(a, b, (((1,), (1,)), ((), ())), preferred_element_type=F32)


def kernel(
    n, mf_hbm, wave, rec, out,
    mf, wave_v, weights, buf_m, buf_c, buf_d, buf_z,
    send_a, send_c, send_x, recv_a, recv_c, recv_x, tile_m, tile_c, tile_z, tile_d,
    rec_v, res, taps_row,
    ssem, rsem, in_sem, out_sem,
):
    span, depth = wave_v.shape[1], wave_v.shape[2]
    pieces = span // STEP
    last = pieces - 1
    early = last * STEP
    cut = span // 2
    half = (mf.shape[1] - 1) // 2
    me = lax.axis_index("shot")
    core = lax.rem(me, 2)
    side = lax.rem(me // 2, 2)
    mate = me + 1 - 2 * core
    across = me + 2 - 4 * side
    cross = across + 1 - 2 * core
    up, down = lax.rem(me + 4, n), lax.rem(me + n - 4, n)
    z_to = (1 - side) * down + side * up
    z_from = (1 - side) * up + side * down
    owner = (core == side)
    giver = (core != side)

    load_taps = pltpu.make_async_copy(mf_hbm, mf, in_sem.at[2])
    load_taps.start()
    load_wave = pltpu.make_async_copy(wave, wave_v, in_sem.at[0])
    load_wave.start()
    load = pltpu.make_async_copy(rec, rec_v, in_sem.at[1])
    load.start()

    barrier = pltpu.get_barrier_semaphore()
    for other in (mate, across, cross, up, down):
        pl.semaphore_signal(barrier, inc=1, device_id={"shot": other}, device_id_type=MESH)
    pl.semaphore_wait(barrier, 5)

    def remote(src, dst, sem, target):
        return pltpu.make_async_remote_copy(
            src_ref=src, dst_ref=dst, send_sem=ssem.at[sem], recv_sem=rsem.at[sem],
            device_id={"shot": target}, device_id_type=MESH,
        )

    def block(src, dst, channel, i, target):
        rows = pl.ds(i * STEP, STEP)
        return remote(src.at[:, rows, :], dst.at[:, rows, :], channel * pieces + i, target)

    def x_copy(i):
        return block(wave, buf_c, CH_X, i, across)

    def z_copy(i):
        return block(wave, buf_z, CH_Z, i, z_to)

    def mate_copy(i):
        return block(wave, buf_m, CH_M, i, mate)

    def share(i):
        return block(buf_c, buf_d, CH_D, i, mate)

    def tile_a(i):
        return block(send_a, recv_a, CH_A, i, z_from)

    def corner(j):
        rows, cols = (
            (pl.ds(0, early), pl.ds(0, early)),
            (pl.ds(0, early), pl.ds(early, STEP)),
            (pl.ds(early, STEP), pl.ds(0, span)),
        )[j]
        return remote(
            send_c.at[:, rows, cols], recv_c.at[:, rows, cols], CH_C * pieces + j, across
        )

    def odd_x():
        rows = pl.ds(0, cut)
        return remote(send_x.at[:, rows, :], recv_x.at[:, rows, :], CH_O * pieces, cross)

    def odd_z():
        rows = pl.ds(cut, span - cut)
        return remote(send_x.at[:, rows, :], recv_x.at[:, rows, :], CH_O * pieces + 1, z_from)

    for i in range(pieces):
        x_copy(i).start()
        z_copy(i).start()
    for i in range(pieces):
        mate_copy(i).start()

    load_taps.wait()
    width = taps_row.shape[1]
    taps_row[...] = jnp.zeros_like(taps_row)
    taps_row[0:2, 0:mf.shape[1]] = mf[...].astype(F32)
    row_id = lax.broadcasted_iota(jnp.int32, (span, width), 0)
    banded = []
    for c in range(2):
        x = jnp.broadcast_to(taps_row[c:c + 1, :], (span, width))
        x = pltpu.roll(x, width - half, 1)
        bit = 1
        while bit < span:
            x = jnp.where((row_id // bit) % 2 == 1, pltpu.roll(x, bit, 1), x)
            bit *= 2
        banded.append(x[:, :span].astype(BF16))
    for j in range(pieces):
        a = banded[0][j * STEP:(j + 1) * STEP]
        b = banded[1][j * STEP:(j + 1) * STEP]
        at = 2 * j * STEP
        weights[0, at:at + STEP, :] = a
        weights[0, at + STEP:at + 2 * STEP, :] = b
        weights[1, at:at + STEP, :] = -b
        weights[1, at + STEP:at + 2 * STEP, :] = a

    def product(left, start, count, right, k):
        a = left[:, start:start + count, :].reshape(2 * count, depth)
        b = right[:, k * STEP:(k + 1) * STEP, :].reshape(2 * STEP, depth)
        y = dot_t(a, b)
        top, low = y[:count], y[count:]
        return top[:, :STEP] - low[:, STEP:], top[:, STEP:] + low[:, :STEP]

    def keep(dst, pair, start, count, k):
        for c in range(2):
            dst[c, start:start + count, k * STEP:(k + 1) * STEP] = pair[c].astype(BF16)

    def flipped(dst, pair, k, skip=0):
        for c in range(2):
            dst[c, k * STEP + skip:(k + 1) * STEP, :] = pair[c].T[skip:].astype(BF16)

    def put(t, k, start, count, j):
        rows = pl.ds(start, count)
        return pltpu.make_async_copy(
            res.at[t, k, :, rows, :], out.at[t, k, :, rows, :], out_sem.at[j]
        )

    def emit(t, k, src, start, count, j):
        rows = slice(start, start + count)
        for p in range(pieces):
            lo, hi = max(p - 1, 0) * STEP, min(p + 2, pieces) * STEP
            cols = slice(p * STEP, (p + 1) * STEP)
            f = sum(
                dot_t(src[c, rows, lo:hi], weights[c, 2 * p * STEP:2 * (p + 1) * STEP, lo:hi])
                for c in range(2)
            )
            res[t, k, 0, rows, cols] = (rec_v[t, k, 0, rows, cols].astype(F32) - f[:, :STEP]).astype(BF16)
            res[t, k, 1, rows, cols] = (rec_v[t, k, 1, rows, cols].astype(F32) - f[:, STEP:]).astype(BF16)
        put(t, k, start, count, j).start()

    load_wave.wait()
    for i in range(pieces):
        mate_copy(i).wait_recv()
        keep(tile_m, product(wave_v, 0, span, buf_m, i), 0, span, i)
    load.wait()
    emit(0, core, tile_m, 0, span, 0)

    for i in range(last):
        x_copy(i).wait_recv()
        share(i).start()
        keep(tile_c, product(wave_v, 0, span, buf_c, i), 0, span, i)
        z_copy(i).wait_recv()
        pair = product(wave_v, 0, span, buf_z, i)
        keep(tile_z, pair, 0, span, i)
        flipped(send_a, pair, i)
    for i in range(last):
        keep(send_c, product(buf_c, 0, early, buf_z, i), 0, early, i)
    corner(0).start()

    x_copy(last).wait_recv()
    share(last).start()
    z_copy(last).wait_recv()
    for i in range(last):
        tile_a(i).start()
    keep(send_c, product(buf_c, 0, early, buf_z, last), 0, early, last)
    corner(1).start()
    pair = product(wave_v, 0, span, buf_z, last)
    flipped(send_a, pair, last)
    tile_a(last).start()
    keep(tile_z, pair, 0, span, last)
    for i in range(pieces):
        keep(send_c, product(buf_c, early, STEP, buf_z, i), early, STEP, i)
    corner(2).start()

    for i in range(pieces):
        share(i).wait_recv()

    @pl.when(owner)
    def _():
        for i in range(pieces):
            pair = product(buf_d, 0, span, buf_z, i)
            for c in range(2):
                send_x[c, :cut, i * STEP:(i + 1) * STEP] = pair[c][:cut].astype(BF16)
            if (i + 1) * STEP > cut:
                flipped(send_x, pair, i, max(cut - i * STEP, 0))
        odd_x().start()
        odd_z().start()

    keep(tile_c, product(wave_v, 0, span, buf_c, last), 0, span, last)
    emit(1, side, tile_c, 0, span, 1)
    emit(2, side, tile_z, 0, span, 2)

    @pl.when(giver)
    def _():
        for i in range(pieces):
            keep(tile_d, product(wave_v, 0, span, buf_d, i), 0, span, i)
        emit(0, 1 - core, tile_d, 0, span, 3)

    corner(0).wait_recv()
    corner(1).wait_recv()
    emit(1, 1 - side, recv_c, 0, early, 4)
    for i in range(last):
        tile_a(i).wait_recv()
        emit(2, 1 - side, recv_a, i * STEP, STEP, 6 + i)
    corner(2).wait_recv()
    emit(1, 1 - side, recv_c, early, STEP, 5)
    tile_a(last).wait_recv()
    emit(2, 1 - side, recv_a, early, STEP, 6 + last)

    @pl.when(owner)
    def _():
        odd_x().wait_recv()
        emit(0, 1 - core, recv_x, 0, cut, 3)
        odd_z().wait_recv()
        emit(0, 1 - core, recv_x, cut, span - cut, 6 + pieces)
        odd_x().wait_send()
        odd_z().wait_send()
        put(0, 1 - core, 0, cut, 3).wait()
        put(0, 1 - core, cut, span - cut, 6 + pieces).wait()

    for i in range(pieces):
        x_copy(i).wait_send()
        z_copy(i).wait_send()
        mate_copy(i).wait_send()
        share(i).wait_send()
        tile_a(i).wait_send()
        put(2, 1 - side, i * STEP, STEP, 6 + i).wait()
    for j in range(3):
        corner(j).wait_send()
    put(0, core, 0, span, 0).wait()
    put(1, side, 0, span, 1).wait()
    put(2, side, 0, span, 2).wait()
    put(1, 1 - side, 0, early, 4).wait()
    put(1, 1 - side, early, STEP, 5).wait()

    @pl.when(giver)
    def _():
        put(0, 1 - core, 0, span, 3).wait()


def ladder(wavefield, recorded, match_filter):
    n = lax.axis_size("shot")
    _, span, depth = wavefield.shape
    pieces = span // STEP
    width = -(-(span + match_filter.shape[1]) // STEP) * STEP
    block = pltpu.VMEM((2, span, depth), BF16)
    flat = pltpu.VMEM((2, span, span), BF16)
    return pl.pallas_call(
        functools.partial(kernel, n),
        out_shape=jax.ShapeDtypeStruct(recorded.shape, recorded.dtype),
        in_specs=[
            pl.BlockSpec(memory_space=pltpu.HBM),
            pl.BlockSpec(memory_space=pltpu.HBM),
            pl.BlockSpec(memory_space=pltpu.HBM),
        ],
        out_specs=pl.BlockSpec(memory_space=pl.ANY),
        scratch_shapes=[
            pltpu.VMEM(match_filter.shape, BF16),
            block,
            pltpu.VMEM((2, 2 * span, span), BF16),
            block, block, block, block,
            flat, flat, flat, flat, flat, flat, flat, flat, flat, flat,
            pltpu.VMEM(recorded.shape, BF16),
            pltpu.VMEM(recorded.shape, BF16),
            pltpu.VMEM((8, width), F32),
            pltpu.SemaphoreType.DMA((7 * pieces,)),
            pltpu.SemaphoreType.DMA((7 * pieces,)),
            pltpu.SemaphoreType.DMA((3,)),
            pltpu.SemaphoreType.DMA((7 + pieces,)),
        ],
        compiler_params=pltpu.CompilerParams(
            collective_id=0, has_side_effects=True, vmem_limit_bytes=LIMIT
        ),
    )(*(pltpu.with_memory_space_constraint(x, pltpu.HBM) for x in (match_filter, wavefield, recorded)))


def passed_along(value, axis, steps):
    count = lax.axis_size(axis)
    pairs = [(source, (source + steps) % count) for source in range(count)]
    return lax.ppermute(value, axis, pairs)


def toeplitz(match_filter, block_span_width):
    tap_count = match_filter.shape[1]
    half_taps = (tap_count - 1) // 2
    row_index = lax.broadcasted_iota(jnp.int32, (block_span_width, block_span_width), 0)
    col_index = lax.broadcasted_iota(jnp.int32, (block_span_width, block_span_width), 1)
    lag_index = row_index - col_index + half_taps
    coeffs = match_filter.astype(jnp.float32)

    def place_tap(tap_index, carried):
        column = lax.dynamic_slice_in_dim(coeffs, tap_index, 1, 1)
        return jnp.where((lag_index == tap_index)[None], column[:, :, None], carried)

    return lax.fori_loop(
        0, tap_count, place_tap, jnp.zeros((2, block_span_width, block_span_width), jnp.float32)
    )


def filter_weights(match_filter, block_span_width):
    toe_pair = toeplitz(match_filter, block_span_width)
    real_component = toe_pair[0].astype(jnp.bfloat16)
    imag_part = toe_pair[1].astype(jnp.bfloat16)
    return jnp.stack(
        [jnp.stack([real_component, imag_part], 1), jnp.stack([-imag_part, real_component], 1)], 0
    )


def shards(wavefield, recorded, match_filter):
    cycle_size = lax.axis_size("shot")
    doubling = cycle_size // 8 == 2 and cycle_size // 4 == 4
    span, taps = wavefield.shape[1], match_filter.shape[1]
    tiled = span % STEP == 0 and span // STEP >= 3 and taps <= 2 * STEP and span % 32 == 0
    if doubling and cycle_size % 4 == 0 and tiled:
        return ladder(wavefield, recorded, match_filter)
    block_span_width = wavefield.shape[1]
    weights = filter_weights(match_filter, block_span_width)
    real_component = wavefield[0]
    imag_part = wavefield[1]
    left_rows = jnp.concatenate(
        [
            jnp.concatenate([real_component, -imag_part], 1),
            jnp.concatenate([imag_part, real_component], 1),
        ],
        0,
    )
    results = []
    for slot_index, offset in enumerate((1, cycle_size // 8, cycle_size // 4)):
        ahead_data = passed_along(wavefield, "shot", -offset)
        right_rows = jnp.concatenate([ahead_data[0], ahead_data[1]], 1)
        stacked = lax.dot_general(
            left_rows, right_rows, (((1,), (1,)), ((), ())), preferred_element_type=jnp.float32
        )
        forward_tile = stacked.astype(jnp.bfloat16).reshape(2, block_span_width, block_span_width)
        ahead_filtered = jnp.einsum(
            "csq,cqdx->dsx", forward_tile, weights, preferred_element_type=jnp.float32
        )
        received = passed_along(forward_tile, "shot", offset)
        behind_filtered = jnp.einsum(
            "csr,csdx->drx", received, weights, preferred_element_type=jnp.float32
        )
        ahead_out = (recorded[slot_index, 0].astype(jnp.float32) - ahead_filtered).astype(
            jnp.bfloat16
        )
        behind_out = (recorded[slot_index, 1].astype(jnp.float32) - behind_filtered).astype(
            jnp.bfloat16
        )
        results.append(jnp.stack([ahead_out, behind_out]))
    return jnp.stack(results)


def solution(mesh):
    return jax.shard_map(
        shards,
        mesh=mesh,
        in_specs=(P("freq", "shot", None), P("freq", None, None, "shot", None), P()),
        out_specs=P("freq", None, None, "shot", None),
        check_vma=False,
    )
```

time: 66.8 us -> 61.9 us (0.927)
  the two profiles are of different devices: /device:TPU:1 before, /device:TPU:0 now
where the time goes in v1:
time: 61.9 us; the launch traced here: 61.7 us
  Pallas kernels  59.9 us (97%)
  local copies, waits for them, and re-layouts  1.8 us (3%)
    pallas_call x1, Pallas kernels, ladder(): pl.pallas_call(functools.partial(kernel, n), out_shape=jax.ShapeDtypeStru...  59.9 us
    unnamed x1, local copies, waits for them, and re-layouts  1.8 us

profile of v1, /device:TPU:0, one launch (start us, length us, event | category | flops | bytes accessed | tf_op | source)
XLA Modules:
  0.0 61.7 jit_solution(854113618803512041)
XLA Ops:
  0.0 59.9 %shard_map.37 = bf16[3,2,2,384,384]{4,3,2,1,0:T(8,128)(2,1)S(1)} custom-call(bf16[2,63]{1,0:T(2,128)(2,1)} %mf_hbm.1, bf16[2,384,1024]{2,1,0:T(8,128)(2,1)} %wave.1, bf16[3,2,2,384,384]{4,3,2,1,0:T(8,128)(2,1)} %rec.1), custom_call_target="tpu_custom_call" | custom-call | tf_op jit(solution)/shard_map/pallas_call | solution.py:272
  59.9 1.8 %copy.5 = bf16[3,2,2,384,384]{4,3,2,1,0:T(8,128)(2,1)} copy(bf16[3,2,2,384,384]{4,3,2,1,0:T(8,128)(2,1)S(1)} %shard_map.37) | data formatting | bytes 7077888

commit v2 on v1

--- a/solution.py
+++ b/solution.py
@@ -9,6 +9,7 @@
 
 MESH = pl.DeviceIdType.MESH
 STEP = 128
+HALF = STEP // 2
 CH_X, CH_Z, CH_M, CH_D, CH_A, CH_C, CH_O = range(7)
 LIMIT = 40 * 2**20
 F32 = jnp.float32
@@ -23,8 +24,8 @@
     n, mf_hbm, wave, rec, out,
     mf, wave_v, weights, buf_m, buf_c, buf_d, buf_z,
     send_a, send_c, send_x, recv_a, recv_c, recv_x, tile_m, tile_c, tile_z, tile_d,
-    rec_v, res, taps_row,
-    ssem, rsem, in_sem, out_sem,
+    rec_v, taps_row,
+    ssem, rsem, in_sem,
 ):
     span, depth = wave_v.shape[1], wave_v.shape[2]
     pieces = span // STEP
@@ -41,6 +42,8 @@
     up, down = lax.rem(me + 4, n), lax.rem(me + n - 4, n)
     z_to = (1 - side) * down + side * up
     z_from = (1 - side) * up + side * down
+    deck = me // 4
+    edge = (deck == 0) | (deck == n // 4 - 1)
     owner = (core == side)
     giver = (core != side)
 
@@ -71,6 +74,10 @@
 
     def z_copy(i):
         return block(wave, buf_z, CH_Z, i, z_to)
+
+    def z_half(j):
+        rows = pl.ds(early + j * HALF, HALF)
+        return remote(wave.at[:, rows, :], buf_z.at[:, rows, :], CH_Z * pieces + last if j == 0 else 7 * pieces, z_to)
 
     def mate_copy(i):
         return block(wave, buf_m, CH_M, i, mate)
@@ -101,7 +108,10 @@
 
     for i in range(pieces):
         x_copy(i).start()
-        z_copy(i).start()
+        if i < last:
+            z_copy(i).start()
+    z_half(0).start()
+    z_half(1).start()
     for i in range(pieces):
         mate_copy(i).start()
 
@@ -143,12 +153,6 @@
         for c in range(2):
             dst[c, k * STEP + skip:(k + 1) * STEP, :] = pair[c].T[skip:].astype(BF16)
 
-    def put(t, k, start, count, j):
-        rows = pl.ds(start, count)
-        return pltpu.make_async_copy(
-            res.at[t, k, :, rows, :], out.at[t, k, :, rows, :], out_sem.at[j]
-        )
-
     def emit(t, k, src, start, count, j):
         rows = slice(start, start + count)
         for p in range(pieces):
@@ -158,9 +162,8 @@
                 dot_t(src[c, rows, lo:hi], weights[c, 2 * p * STEP:2 * (p + 1) * STEP, lo:hi])
                 for c in range(2)
             )
-            res[t, k, 0, rows, cols] = (rec_v[t, k, 0, rows, cols].astype(F32) - f[:, :STEP]).astype(BF16)
-            res[t, k, 1, rows, cols] = (rec_v[t, k, 1, rows, cols].astype(F32) - f[:, STEP:]).astype(BF16)
-        put(t, k, start, count, j).start()
+            out[t, k, 0, rows, cols] = (rec_v[t, k, 0, rows, cols].astype(F32) - f[:, :STEP]).astype(BF16)
+            out[t, k, 1, rows, cols] = (rec_v[t, k, 1, rows, cols].astype(F32) - f[:, STEP:]).astype(BF16)
 
     load_wave.wait()
     for i in range(pieces):
@@ -177,15 +180,21 @@
         pair = product(wave_v, 0, span, buf_z, i)
         keep(tile_z, pair, 0, span, i)
         flipped(send_a, pair, i)
+        pl.when(edge)(tile_a(i).start)
     for i in range(last):
         keep(send_c, product(buf_c, 0, early, buf_z, i), 0, early, i)
     corner(0).start()
 
     x_copy(last).wait_recv()
     share(last).start()
-    z_copy(last).wait_recv()
-    for i in range(last):
-        tile_a(i).start()
+    z_half(0).wait_recv()
+
+    @pl.when(jnp.logical_not(edge))
+    def _():
+        for i in range(last):
+            tile_a(i).start()
+
+    z_half(1).wait_recv()
     keep(send_c, product(buf_c, 0, early, buf_z, last), 0, early, last)
     corner(1).start()
     pair = product(wave_v, 0, span, buf_z, last)
@@ -239,27 +248,30 @@
         emit(0, 1 - core, recv_x, cut, span - cut, 6 + pieces)
         odd_x().wait_send()
         odd_z().wait_send()
-        put(0, 1 - core, 0, cut, 3).wait()
-        put(0, 1 - core, cut, span - cut, 6 + pieces).wait()
+        pass
+        pass
 
     for i in range(pieces):
         x_copy(i).wait_send()
-        z_copy(i).wait_send()
+        if i < last:
+            z_copy(i).wait_send()
         mate_copy(i).wait_send()
         share(i).wait_send()
         tile_a(i).wait_send()
-        put(2, 1 - side, i * STEP, STEP, 6 + i).wait()
+        pass
+    z_half(0).wait_send()
+    z_half(1).wait_send()
     for j in range(3):
         corner(j).wait_send()
-    put(0, core, 0, span, 0).wait()
-    put(1, side, 0, span, 1).wait()
-    put(2, side, 0, span, 2).wait()
-    put(1, 1 - side, 0, early, 4).wait()
-    put(1, 1 - side, early, STEP, 5).wait()
+    pass
+    pass
+    pass
+    pass
+    pass
 
     @pl.when(giver)
     def _():
-        put(0, 1 - core, 0, span, 3).wait()
+        pass
 
 
 def ladder(wavefield, recorded, match_filter):
@@ -277,7 +289,7 @@
             pl.BlockSpec(memory_space=pltpu.HBM),
             pl.BlockSpec(memory_space=pltpu.HBM),
         ],
-        out_specs=pl.BlockSpec(memory_space=pl.ANY),
+        out_specs=pl.BlockSpec(memory_space=pltpu.VMEM),
         scratch_shapes=[
             pltpu.VMEM(match_filter.shape, BF16),
             block,
@@ -285,12 +297,10 @@
             block, block, block, block,
             flat, flat, flat, flat, flat, flat, flat, flat, flat, flat,
             pltpu.VMEM(recorded.shape, BF16),
-            pltpu.VMEM(recorded.shape, BF16),
             pltpu.VMEM((8, width), F32),
-            pltpu.SemaphoreType.DMA((7 * pieces,)),
-            pltpu.SemaphoreType.DMA((7 * pieces,)),
+            pltpu.SemaphoreType.DMA((7 * pieces + 1,)),
+            pltpu.SemaphoreType.DMA((7 * pieces + 1,)),
             pltpu.SemaphoreType.DMA((3,)),
-            pltpu.SemaphoreType.DMA((7 + pieces,)),
         ],
         compiler_params=pltpu.CompilerParams(
             collective_id=0, has_side_effects=True, vmem_limit_bytes=LIMIT

time: 61.9 us -> 60.1 us (0.971)
  Pallas kernels: 59.9 us -> 58.2 us
    pallas_call x1, Pallas kernels: 59.9 us -> 58.2 us  [ladder(): pl.pallas_call(functools.partial(kernel, n), out_shape=jax.ShapeDtypeStru...]
where the time goes in v2:
time: 60.1 us; the launch traced here: 60 us
  Pallas kernels  58.2 us (97%)
  local copies, waits for them, and re-layouts  1.8 us (3%)
    pallas_call x1, Pallas kernels, ladder(): pl.pallas_call(functools.partial(kernel, n), out_shape=jax.ShapeDtypeStru...  58.2 us
    unnamed x1, local copies, waits for them, and re-layouts  1.8 us

profile of v2, /device:TPU:0, one launch (start us, length us, event | category | flops | bytes accessed | tf_op | source)
XLA Modules:
  0.0 60.0 jit_solution(17566228009195609019)
XLA Ops:
  0.0 58.2 %shard_map.37 = bf16[3,2,2,384,384]{4,3,2,1,0:T(8,128)(2,1)S(1)} custom-call(bf16[2,63]{1,0:T(2,128)(2,1)} %mf_hbm.1, bf16[2,384,1024]{2,1,0:T(8,128)(2,1)} %wave.1, bf16[3,2,2,384,384]{4,3,2,1,0:T(8,128)(2,1)} %rec.1), custom_call_target="tpu_custom_call" | custom-call | tf_op jit(solution)/shard_map/pallas_call | solution.py:284
  58.2 1.8 %copy.5 = bf16[3,2,2,384,384]{4,3,2,1,0:T(8,128)(2,1)} copy(bf16[3,2,2,384,384]{4,3,2,1,0:T(8,128)(2,1)S(1)} %shard_map.37) | data formatting | bytes 7077888

commit v3 on v2

--- a/solution.py
+++ b/solution.py
@@ -102,9 +102,11 @@
         rows = pl.ds(0, cut)
         return remote(send_x.at[:, rows, :], recv_x.at[:, rows, :], CH_O * pieces, cross)
 
-    def odd_z():
-        rows = pl.ds(cut, span - cut)
-        return remote(send_x.at[:, rows, :], recv_x.at[:, rows, :], CH_O * pieces + 1, z_from)
+    def odd_z(j):
+        rows = pl.ds(cut, early - cut) if j == 0 else pl.ds(early, STEP)
+        return remote(
+            send_x.at[:, rows, :], recv_x.at[:, rows, :], CH_O * pieces + 1 + j, z_from
+        )
 
     for i in range(pieces):
         x_copy(i).start()
@@ -217,7 +219,8 @@
             if (i + 1) * STEP > cut:
                 flipped(send_x, pair, i, max(cut - i * STEP, 0))
         odd_x().start()
-        odd_z().start()
+        odd_z(0).start()
+        odd_z(1).start()
 
     keep(tile_c, product(wave_v, 0, span, buf_c, last), 0, span, last)
     emit(1, side, tile_c, 0, span, 1)
@@ -244,10 +247,13 @@
     def _():
         odd_x().wait_recv()
         emit(0, 1 - core, recv_x, 0, cut, 3)
-        odd_z().wait_recv()
-        emit(0, 1 - core, recv_x, cut, span - cut, 6 + pieces)
+        odd_z(0).wait_recv()
+        emit(0, 1 - core, recv_x, cut, early - cut, 6 + pieces)
+        odd_z(1).wait_recv()
+        emit(0, 1 - core, recv_x, early, STEP, 6 + pieces)
         odd_x().wait_send()
-        odd_z().wait_send()
+        odd_z(0).wait_send()
+        odd_z(1).wait_send()
         pass
         pass
 

time: 60.1 us -> 60.4 us (level)
  no operation moved by 1% of the time
where the time goes in v3:
time: 60.4 us; the launch traced here: 60.3 us
  Pallas kernels  58.5 us (97%)
  local copies, waits for them, and re-layouts  1.8 us (3%)
    pallas_call x1, Pallas kernels, ladder(): pl.pallas_call(functools.partial(kernel, n), out_shape=jax.ShapeDtypeStru...  58.5 us
    unnamed x1, local copies, waits for them, and re-layouts  1.8 us

profile of v3, /device:TPU:0, one launch (start us, length us, event | category | flops | bytes accessed | tf_op | source)
XLA Modules:
  0.0 60.3 jit_solution(5384085247409905805)
XLA Ops:
  0.0 58.5 %shard_map.37 = bf16[3,2,2,384,384]{4,3,2,1,0:T(8,128)(2,1)S(1)} custom-call(bf16[2,63]{1,0:T(2,128)(2,1)} %mf_hbm.1, bf16[2,384,1024]{2,1,0:T(8,128)(2,1)} %wave.1, bf16[3,2,2,384,384]{4,3,2,1,0:T(8,128)(2,1)} %rec.1), custom_call_target="tpu_custom_call" | custom-call | tf_op jit(solution)/shard_map/pallas_call | solution.py:290
  58.5 1.8 %copy.5 = bf16[3,2,2,384,384]{4,3,2,1,0:T(8,128)(2,1)} copy(bf16[3,2,2,384,384]{4,3,2,1,0:T(8,128)(2,1)S(1)} %shard_map.37) | data formatting | bytes 7077888
